TPU v7x, 512 devices: a whole 4x8x8 slice. The times are simulated.
512 devices in a mesh: dom: 128 (over z, y, core), sub: 4 (over x).
Axes of the slice: x: 4, y: 8, z: 8, core: 2. Of those that a mesh axis runs over, the one named last changes fastest.
Arguments:
- source: float32 [512, 7, 16, 1024], P('dom', None, 'sub'), may hold values from -6 to 6
- zone_ids: int32 [512, 1024], P('dom'), may hold values from 0 to 15
- kappa_table: float32 [16, 7], replicated, may hold values from 0.05 to 1
- mu_table: float32 [16, 8], replicated, may hold values from 0.2 to 2
- owner_dev: int32 [128, 32], P('dom'), may hold values from 0 to 127, as said below
- owner_group: int32 [128, 128], P('dom'), may hold values from 0 to 127, as said below
Outputs:
- edge_field: float32 [512, 7, 16, 1024], P('dom', None, 'sub')
- potential: float32 [512, 16, 1024], P('dom', 'sub')
Inputs may be any that keep to these rules, and one draw needn't show every extreme that they name: owner_dev[d, j] is the index along dom of the device that sums slot j of device d; one device sends at most 1 of its slots to one owner, and exactly 1 to some owner. At owner e, receive position d + c stands for the c-th slot, in slot order, that device d sends to e. owner_group[e, d + c] is a receive position held alike by all copies of one shared primitive; a primitive has at most four copies, all at one owner; positions that no slot reaches hold their own index.
All inputs are finite; a program needn't handle non-finite values.
Results may differ from a plain program's by a relative error of at most 0.0001.
Values sent between devices are 32-bit elements; how exact they have to be, the bound alone decides.
A program may use at most 64 MiB of HBM per device.

v0:
```python
import functools

import jax
import jax.numpy as jnp
from jax import lax
from jax.experimental import pallas as pl
from jax.experimental.pallas import tpu as pltpu
from jax.sharding import PartitionSpec as P

MESH = pl.DeviceIdType.MESH
LAT = 32
PLANES = 4
CORES = 2
EDGE_DAMPING = 0.6
NODE_DAMPING = 0.8
POS = {0: 0, 1: 1, 3: 2, 2: 3, 4: 4, 5: 5, 6: 6}
FLAT_TYPES = (0, 1, 3)
SHARED = (1, 2, 5)
PRIVATE = (0, 3, 4, 6)
TILE = (8, 128)


class Lanes:
    def __init__(self):
        self.lane = lax.broadcasted_iota(jnp.int32, TILE, 1)
        self.sub = lax.broadcasted_iota(jnp.int32, TILE, 0)
        self.x = self.lane % LAT
        self.left = self.x == 0
        self.right = self.x == LAT - 1
        self.last_y = (self.sub == 7) & (self.lane >= 96)
        self.first_y = (self.sub == 0) & (self.lane < 32)

    def side(self, s):
        return self.right if s else self.left

    def ax(self, v):
        return jnp.where(self.right, 0.0, pltpu.roll(v, 127, 1))

    def bx(self, v):
        return jnp.where(self.left, 0.0, pltpu.roll(v, 1, 1))

    def ay(self, v):
        r = pltpu.roll(v, 96, 1)
        r = jnp.where(self.lane < 96, r, pltpu.roll(r, 7, 0))
        return jnp.where(self.last_y, 0.0, r)

    def by(self, v):
        r = pltpu.roll(v, 32, 1)
        r = jnp.where(self.lane >= 32, r, pltpu.roll(r, 1, 0))
        return jnp.where(self.first_y, 0.0, r)

    def pack(self, v, s, idx):
        return pltpu.roll(jnp.where(self.side(s), v, 0.0), (idx - s * (LAT - 1) + 128) % 128, 1)

    def unpack(self, v, s, idx):
        return pltpu.roll(v, (s * (LAT - 1) - idx + 128) % 128, 1)


class Gather:
    def __init__(self, buf, sems, me, side):
        self.buf, self.sems = buf, sems
        self.side = side
        self.core, self.a, self.b, self.k, self.dev = me
        self.sent = []

    def row(self):
        return (self.core * self.side + self.a) * self.side + self.b

    def line(self, core, a):
        return self.buf.at[pl.ds((core * self.side + a) * self.side, self.side)]

    def send(self, stage, i, ref, target):
        copy = pltpu.make_async_remote_copy(
            src_ref=ref,
            dst_ref=ref,
            send_sem=self.sems.at[stage, 0, i],
            recv_sem=self.sems.at[stage, 1, i],
            device_id=target,
            device_id_type=MESH,
        )
        copy.start()
        self.sent.append(copy)

    def arrived(self, stage, i, ref):
        pltpu.make_async_remote_copy(
            src_ref=ref,
            dst_ref=ref,
            send_sem=self.sems.at[stage, 0, i],
            recv_sem=self.sems.at[stage, 1, i],
            device_id=self.dev(self.core, self.a, self.b),
            device_id_type=MESH,
        ).wait_recv()

    def first(self):
        ref = self.buf.at[self.row()]
        for i in range(1, self.side):
            self.send(0, i, ref, self.dev(self.core, self.a, (self.b + i) % self.side))

    def second(self):
        for i in range(1, self.side):
            source = (self.b - i + self.side) % self.side
            self.arrived(0, i, self.buf.at[(self.core * self.side + self.a) * self.side + source])
        ref = self.line(self.core, self.a)
        for i in range(1, self.side):
            self.send(1, i, ref, self.dev(self.core, (self.a + i) % self.side, self.b))
        self.send(2, 0, ref, self.dev(1 - self.core, self.b, self.a))

    def third(self):
        for i in range(1, self.side):
            ref = self.line(self.core, (self.a - i + self.side) % self.side)
            self.arrived(1, i, ref)
            self.send(2, i, ref, self.dev(1 - self.core, self.b, self.a))

    def finish(self):
        for i in range(self.side):
            self.arrived(2, i, self.line(1 - self.core, (self.b - i + self.side) % self.side))

    def drain(self):
        for copy in self.sent:
            copy.wait_send()


def kernel(
    side, n_sub, macros, zones,
    src, zone, od_s, od_v, og_v, kappa, mu,
    out_e, out_p,
    S, EF, R, SB, SA, RB, RA, NR, NB, NA, C1, C2,
    MC, INVH, INV0, INVS, NDH, ND0, ND,
    G0, G1, G2, G3, GI, HS, HR,
    ODS, GRS, JS, IDXV, IDXS,
    gsem, bsem, hsem, isem,
):
    dom = lax.axis_index("dom")
    k = lax.axis_index("sub")
    core = dom % CORES
    zc = dom // (CORES * side)
    yc = (dom // CORES) % side
    a = jnp.where(core == 0, zc, yc)
    b = jnp.where(core == 0, yc, zc)

    def dev(core_, a_, b_):
        z_ = jnp.where(core_ == 0, a_, b_)
        y_ = jnp.where(core_ == 0, b_, a_)
        return ((z_ * side + y_) * CORES + core_, k)

    me = (core, a, b, k, dev)
    barrier = pltpu.get_barrier_semaphore()

    def greet(target):
        pl.semaphore_signal(barrier, inc=1, device_id=target, device_id_type=MESH)

    for i in range(1, side):
        greet(dev(core, a, (b + i) % side))
        greet(dev(core, (a + i) % side, b))
    greet(dev(1 - core, b, a))
    has_up = k < n_sub - 1
    has_down = k > 0

    @pl.when(has_up)
    def _():
        greet((dom, k + 1))

    @pl.when(has_down)
    def _():
        greet((dom, k - 1))

    ln = Lanes()
    ahead = {0: ln.ax, 1: ln.ay, 3: lambda v: ln.ax(ln.ay(v))}
    behind = {0: ln.bx, 1: ln.by, 3: lambda v: ln.bx(ln.by(v))}
    zero = jnp.zeros(TILE, jnp.float32)
    inside0 = jnp.where(has_down, 1.0, 0.0)

    nd_dev = side * side * CORES
    for buf in (G0, G1, G2, G3):
        for u in range(buf.shape[1]):
            buf[nd_dev, u] = zero

    gi = Gather(GI, gsem.at[4], me, side)
    g0 = Gather(G0, gsem.at[0], me, side)
    g1 = Gather(G1, gsem.at[1], me, side)
    g2 = Gather(G2, gsem.at[2], me, side)
    g3 = Gather(G3, gsem.at[3], me, side)
    row = gi.row()

    GI[row] = jnp.full(TILE, -1, jnp.int32)
    GI[row, 0:1, 0 : og_v.shape[1]] = og_v[...]
    GI[row, 1:2, 0 : od_v.shape[1]] = od_v[...]

    def prepare(m, packs):
        zid = zone[m]
        hits = [zid == zz for zz in range(zones)]
        mass, curl = [], []
        for t in range(7):
            v = zero
            for zz in range(zones):
                v = jnp.where(hits[zz], kappa[t, zz], v)
            mass.append(v)
            MC[m, t] = v
        for f in range(8):
            v = zero
            for zz in range(zones):
                v = jnp.where(hits[zz], mu[f, zz], v)
            curl.append(v)
            MC[m, 7 + f] = v
        diag = {
            0: mass[0] + curl[0] + curl[2] + behind[1](curl[1]),
            1: mass[1] + curl[1] + curl[4] + behind[0](curl[0]),
            2: mass[2] + curl[3] + curl[5] + curl[7] + behind[0](curl[2]) + behind[1](curl[4]) + behind[3](curl[6]),
            3: mass[3] + curl[0] + curl[1] + curl[6],
            4: mass[4] + curl[2] + curl[3],
            5: mass[5] + curl[4] + curl[5],
            6: mass[6] + curl[6] + curl[7],
        }
        low = {0: curl[3], 1: curl[5], 3: curl[7]}
        node = functools.reduce(lambda p, q: p + q, mass) + behind[0](mass[0]) + behind[1](mass[1]) + behind[3](mass[3])
        node_low = mass[2] + behind[0](mass[4]) + behind[1](mass[5]) + behind[3](mass[6])
        full = {t: diag[t] + low[t] if t in low else diag[t] for t in range(7)}
        first = {t: diag[t] + inside0 * low[t] if t in low else diag[t] for t in range(7)}
        for t in range(7):
            INVH[m, POS[t]] = EDGE_DAMPING / full[t]
        for n, t in enumerate(FLAT_TYPES):
            INV0[m, n] = EDGE_DAMPING / first[t]
        for n, t in enumerate(SHARED):
            INVS[m, n, 0] = first[t]
            for p in range(1, PLANES):
                INVS[m, n, p] = full[t]
        node_full, node_first = node + node_low, node + inside0 * node_low
        NDH[m] = NODE_DAMPING / node_full
        ND[m, 0] = node_first
        for p in range(1, PLANES):
            ND[m, p] = node_full
        for t in range(7):
            for p in range(PLANES):
                S[m, POS[t], p] = src[m, t, :, p, :]
        packs = list(packs)
        for s in range(2):
            for n, t in enumerate(SHARED):
                for p in range(PLANES):
                    packs[n] = packs[n] + ln.pack(S[m, POS[t], p], s, (m * 2 + s) * 4 + p)
            for n, (f_, g_) in enumerate([(full[t], first[t]) for t in SHARED] + [(node_full, node_first)]):
                packs[3] = packs[3] + ln.pack(f_, s, (m * 2 + s) * 4 + n)
                packs[4] = packs[4] + ln.pack(g_, s, (m * 2 + s) * 4 + n)
        return tuple(packs)

    packs = lax.fori_loop(0, macros, prepare, (zero,) * 5)
    for u in range(5):
        G0[row, u] = packs[u]

    pl.semaphore_wait(
        barrier, 2 * (side - 1) + 1 + jnp.where(has_up, 1, 0) + jnp.where(has_down, 1, 0)
    )
    gi.first()
    g0.first()

    def vertical(direction, source, target, sems, i):
        step = 1 - 2 * direction
        return pltpu.make_async_remote_copy(
            src_ref=source,
            dst_ref=target,
            send_sem=sems.at[i, direction, 0],
            recv_sem=sems.at[i, direction, 1],
            device_id=(dom, k + step),
            device_id_type=MESH,
        )

    pending = []

    def push(direction, source, target, sems, i):
        copy = vertical(direction, source, target, sems, i)
        able = has_down if direction else has_up
        pending.append((copy, able))

        @pl.when(able)
        def _():
            copy.start()

        return copy

    def pull(direction, source, target, sems, i):
        copy = vertical(direction, source, target, sems, i)

        @pl.when(has_up if direction else has_down)
        def _():
            copy.wait_recv()

    @pl.when(jnp.logical_not(has_down))
    def _():
        SB[...] = jnp.zeros_like(SB)
        RB[...] = jnp.zeros_like(RB)
        NB[...] = jnp.zeros_like(NB)
        for i in range(4):
            HR[i, 0] = zero

    @pl.when(jnp.logical_not(has_up))
    def _():
        SA[...] = jnp.zeros_like(SA)
        RA[...] = jnp.zeros_like(RA)
        NA[...] = jnp.zeros_like(NA)
        for i in range(4):
            HR[i, 1] = zero

    s_up = (0, S.at[:, :, PLANES - 1], SB, bsem, 0)
    s_down = (1, S.at[:, 0:3, 0], SA, bsem, 0)
    push(*s_up)
    push(*s_down)

    def inverse(m, t, p):
        if p == 0 and t in FLAT_TYPES:
            return INV0[m, POS[t]]
        return INVH[m, POS[t]]

    def start_private(m, carry):
        for t in PRIVATE:
            for p in range(PLANES):
                EF[m, POS[t], p + 1] = inverse(m, t, p) * S[m, POS[t], p]
        return carry

    lax.fori_loop(0, macros, start_private, 0)
    gi.second()
    g0.second()
    gi.third()
    gi.finish()

    def place(r, carry):
        c_ = r // (side * side)
        a_ = (r // side) % side
        b_ = r % side
        natural = jnp.where(c_ == 0, a_ * side + b_, b_ * side + a_) * CORES + c_
        ODS[pl.ds(natural, 1), :] = GI[r, 1:2, :]
        return carry

    ODS[...] = jnp.full(ODS.shape, -1, jnp.int32)
    lax.fori_loop(0, nd_dev, place, 0)
    slots = od_v.shape[1]
    owners = jnp.transpose(ODS[...])[0:slots]
    number = lax.broadcasted_iota(jnp.int32, owners.shape, 0) + 1

    def look(j, carry):
        e = od_s[0, j]
        c_ = e % CORES
        z_ = e // (CORES * side)
        y_ = (e // CORES) % side
        r = c_ * side * side + jnp.where(c_ == 0, z_ * side + y_, y_ * side + z_)
        GRS[pl.ds(j, 1), :] = GI[r, 0:1, :]
        hit = jnp.where(owners == e, number, 0)
        JS[pl.ds(j, 1), :] = jnp.max(hit, axis=0, keepdims=True)
        return carry

    lax.fori_loop(0, slots, look, 0)
    group, place_of = GRS[...], JS[...]
    device = lax.broadcasted_iota(jnp.int32, group.shape, 1)
    c_ = device % CORES
    z_ = device // (CORES * side)
    y_ = (device // CORES) % side
    rows = (c_ * side * side + jnp.where(c_ == 0, z_ * side + y_, y_ * side + z_))
    mine = jnp.max(jnp.where(device == dom, group, -2), axis=1, keepdims=True)
    mate = (group == mine) & (place_of > 0) & (device != dom)
    none = nd_dev * 32
    code = jnp.where(mate, rows * 32 + place_of - 1, none)
    found = jnp.zeros(group.shape, jnp.int32)
    for i in range(3):
        least = jnp.min(code, axis=1, keepdims=True)
        found = jnp.where(device == i, least, found)
        code = jnp.where(code == least, none, code)
    IDXV[...] = jnp.clip(found, 0, none)
    to_scalar = pltpu.make_async_copy(IDXV, IDXS, isem)
    to_scalar.start()
    to_scalar.wait()

    g0.third()
    g0.finish()

    def others(buf, units, m, p, s):
        j = (m * 2 + s) * 4 + p
        totals = [None] * len(units)
        for i in range(3):
            code = IDXS[j, i]
            r = jnp.clip(code // 32, 0, nd_dev)
            theirs = code % 32
            for n, u in enumerate(units):
                v = ln.unpack(buf[r, u], s, theirs)
                totals[n] = v if totals[n] is None else totals[n] + v
        return totals

    def others_diag(m, p, s):
        j = (m * 2 + s) * 4 + p
        totals = [None] * 4
        for i in range(3):
            code = IDXS[j, i]
            r = jnp.clip(code // 32, 0, nd_dev)
            theirs = code % 32
            low = theirs % 4
            v0 = G0[r, jnp.where(low == 0, 4, 3)]
            for n in range(4):
                v = ln.unpack(v0, s, theirs - low + n)
                totals[n] = v if totals[n] is None else totals[n] + v
        return totals

    def assembled(buf, units, m, p, values):
        for s in range(2):
            extra = others(buf, units, m, p, s)
            values = [jnp.where(ln.side(s), v + e, v) for v, e in zip(values, extra)]
        return values

    def start_shared(m, carry):
        up, down = carry
        for p in range(PLANES):
            values = assembled(G0, (0, 1, 2), m, p, [S[m, POS[t], p] for t in SHARED])
            diags = [INVS[m, n, p] for n in range(3)] + [ND[m, p]]
            for s in range(2):
                extra = others_diag(m, p, s)
                diags = [jnp.where(ln.side(s), v + e, v) for v, e in zip(diags, extra)]
            ND[m, p] = NODE_DAMPING / diags[3]
            for n, t in enumerate(SHARED):
                inv = EDGE_DAMPING / diags[n]
                INVS[m, n, p] = inv
                new = inv * values[n]
                EF[m, POS[t], p + 1] = new
                for s in range(2):
                    if p == PLANES - 1:
                        up = up + ln.pack(new, s, (m * 2 + s) * 4 + n)
                    if p == 0 and t == 1:
                        down = down + ln.pack(new, s, (m * 2 + s) * 4 + n)
        return up, down

    def send_sides(event, up, down, both=True):
        if both:
            HS[event, 0] = up
            push(0, HS.at[event, 0], HR.at[event, 0], hsem, event)
        HS[event, 1] = down
        push(1, HS.at[event, 1], HR.at[event, 1], hsem, event)

    def take_sides(event, both=True):
        if both:
            pull(0, HS.at[event, 0], HR.at[event, 0], hsem, event)
        pull(1, HS.at[event, 1], HR.at[event, 1], hsem, event)

    def replace(v, packed, m, n):
        for s in range(2):
            v = jnp.where(ln.side(s), ln.unpack(packed, s, (m * 2 + s) * 4 + n), v)
        return v

    up, down = lax.fori_loop(0, macros, start_shared, (zero, zero))
    send_sides(0, up, down)
    pull(*s_up)
    pull(*s_down)
    take_sides(0)

    def halo_edges(event, below, above, fresh):
        def body(m, carry):
            from_below, from_above = HR[event, 0], HR[event, 1]
            for t in range(7):
                v = INVH[m, POS[t]] * below[m, POS[t]]
                if not fresh:
                    v = EF[m, POS[t], 0] + v
                if t in SHARED:
                    v = replace(v, from_below, m, SHARED.index(t))
                EF[m, POS[t], 0] = v
            for t in FLAT_TYPES:
                v = INVH[m, POS[t]] * above[m, POS[t]]
                if not fresh:
                    v = EF[m, POS[t], PLANES + 1] + v
                if t in SHARED:
                    v = replace(v, from_above, m, 0)
                EF[m, POS[t], PLANES + 1] = v
            return carry

        lax.fori_loop(0, macros, body, 0)

    halo_edges(0, SB, SA, True)

    def operate(m, want_nodes, sink):
        mass = [MC[m, t] for t in range(7)]
        curl = [MC[m, 7 + f] for f in range(8)]
        w3b = w5b = w7b = None
        rb = None
        for z in range(-1, PLANES):
            u = {t: EF[m, POS[t], z + 1] for t in range(7)}
            n = {t: EF[m, POS[t], z + 2] for t in FLAT_TYPES}
            w3 = curl[3] * (u[2] + n[0] - u[4])
            w5 = curl[5] * (u[2] + n[1] - u[5])
            w7 = curl[7] * (u[2] + n[3] - u[6])
            if z == -1:
                w3, w5, w7 = inside0 * w3, inside0 * w5, inside0 * w7
            if z >= 0 or want_nodes:
                ay2 = ln.ay(u[2])
                w2 = curl[2] * (u[0] + ln.ax(u[2]) - u[4])
                w4 = curl[4] * (u[1] + ay2 - u[5])
                w6 = curl[6] * (u[3] + ln.ax(ay2) - u[6])

                def given(t):
                    return SB[m, POS[t]] if z < 0 else S[m, POS[t], z]

                r = {
                    2: given(2) - (mass[2] * u[2] + (w3 + w5 + w7) + ln.bx(w2 + ln.by(w6)) + ln.by(w4)),
                    4: given(4) - (mass[4] * u[4] - w2 - w3),
                    5: given(5) - (mass[5] * u[5] - w4 - w5),
                    6: given(6) - (mass[6] * u[6] - w6 - w7),
                }
                if z >= 0:
                    w0 = curl[0] * (u[0] + ln.ax(u[1]) - u[3])
                    w1 = curl[1] * (u[1] + ln.ay(u[0]) - u[3])
                    r[0] = given(0) - (mass[0] * u[0] + w0 + w2 + ln.by(w1) + w3b)
                    r[1] = given(1) - (mass[1] * u[1] + w1 + w4 + ln.bx(w0) + w5b)
                    r[3] = given(3) - (mass[3] * u[3] - w0 - w1 + w6 + w7b)
                    sink(z, r, rb)
                rb = r
            w3b, w5b, w7b = w3, w5, w7

    def node_stage(sweep):
        def body(m, pack):
            box = [pack]

            def sink(z, r, rb):
                total = ln.bx(r[0] + rb[4] + ln.by(r[3] + rb[6])) + ln.by(r[1] + rb[5]) + rb[2]
                own = ((r[0] + r[1]) + (r[2] + r[3])) + ((r[4] + r[5]) + r[6])
                node = total - own
                NR[sweep, m, z] = node
                for s in range(2):
                    box[0] = box[0] + ln.pack(node, s, (m * 2 + s) * 4 + z)

            operate(m, True, sink)
            return box[0]

        return lax.fori_loop(0, macros, body, zero)

    def node_round(sweep, gather, buf, corr, both):
        buf[row, 0] = node_stage(sweep)
        gather.first()
        n_up = (0, NR.at[sweep, :, PLANES - 1], NB, bsem, 1 + 2 * sweep)
        n_down = (1, NR.at[sweep, :, 0], NA.at[sweep], bsem, 1 + 2 * sweep)
        if both:
            push(*n_up)
        push(*n_down)
        gather.second()
        gather.third()
        gather.finish()

        def correct(m, carry):
            up_, down_ = carry
            for p in range(PLANES):
                (value,) = assembled(buf, (0,), m, p, [NR[sweep, m, p]])
                value = ND[m, p] * value
                corr[m, p + 1] = value
                for s in range(2):
                    if p == PLANES - 1:
                        up_ = up_ + ln.pack(value, s, (m * 2 + s) * 4)
                    if p == 0:
                        down_ = down_ + ln.pack(value, s, (m * 2 + s) * 4)
            return up_, down_

        up_, down_ = lax.fori_loop(0, macros, correct, (zero, zero))
        event = 1 + 2 * sweep
        send_sides(event, up_, down_, both)
        if both:
            pull(*n_up)
        pull(*n_down)
        take_sides(event, both)

        def halo(m, carry):
            if both:
                corr[m, 0] = replace(NDH[m] * NB[m], HR[event, 0], m, 0)
            corr[m, PLANES + 1] = replace(NDH[m] * NA[sweep, m], HR[event, 1], m, 0)
            return carry

        lax.fori_loop(0, macros, halo, 0)

    def raised(corr, m, z, t):
        dz = 0 if t in FLAT_TYPES else 1
        flat = {0: 0, 1: 1, 3: 3, 2: None, 4: 0, 5: 1, 6: 3}[t]
        v = corr[m, z + 1 + dz]
        if flat is not None:
            v = ahead[flat](v)
        return v - corr[m, z + 1]

    node_round(0, g1, G1, C1, True)

    def raise_all(m, carry):
        for t in range(7):
            for z in range(-1, PLANES):
                step = raised(C1, m, z, t)
                EF[m, POS[t], z + 1] = EF[m, POS[t], z + 1] + (inside0 * step if z < 0 else step)
        for t in FLAT_TYPES:
            EF[m, POS[t], PLANES + 1] = EF[m, POS[t], PLANES + 1] + raised(C1, m, PLANES, t)
        return carry

    lax.fori_loop(0, macros, raise_all, 0)

    def residual_stage(m, packs):
        box = list(packs)

        def sink(z, r, rb):
            for t in range(7):
                R[m, POS[t], z] = r[t]
            for n, t in enumerate(SHARED):
                for s in range(2):
                    box[n] = box[n] + ln.pack(r[t], s, (m * 2 + s) * 4 + z)

        operate(m, False, sink)
        return tuple(box)

    packs = lax.fori_loop(0, macros, residual_stage, (zero,) * 3)
    for u in range(3):
        G2[row, u] = packs[u]
    g2.first()
    r_up = (0, R.at[:, :, PLANES - 1], RB, bsem, 2)
    r_down = (1, R.at[:, 0:3, 0], RA, bsem, 2)
    push(*r_up)
    push(*r_down)

    def second_private(m, carry):
        for t in PRIVATE:
            for p in range(PLANES):
                EF[m, POS[t], p + 1] = EF[m, POS[t], p + 1] + inverse(m, t, p) * R[m, POS[t], p]
        return carry

    lax.fori_loop(0, macros, second_private, 0)
    g2.second()
    g2.third()
    g2.finish()

    def second_shared(m, carry):
        up, down = carry
        for p in range(PLANES):
            values = assembled(G2, (0, 1, 2), m, p, [R[m, POS[t], p] for t in SHARED])
            for n, t in enumerate(SHARED):
                new = EF[m, POS[t], p + 1] + INVS[m, n, p] * values[n]
                EF[m, POS[t], p + 1] = new
                for s in range(2):
                    if p == PLANES - 1:
                        up = up + ln.pack(new, s, (m * 2 + s) * 4 + n)
                    if p == 0 and t == 1:
                        down = down + ln.pack(new, s, (m * 2 + s) * 4 + n)
        return up, down

    up, down = lax.fori_loop(0, macros, second_shared, (zero, zero))
    send_sides(2, up, down)
    pull(*r_up)
    pull(*r_down)
    take_sides(2)
    halo_edges(2, RB, RA, False)
    node_round(1, g3, G3, C2, False)

    def finish(m, carry):
        for t in range(7):
            for z in range(PLANES):
                out_e[m, t, :, z, :] = EF[m, POS[t], z + 1] + raised(C2, m, z, t)
        for z in range(PLANES):
            out_p[m, :, z, :] = C1[m, z + 1] + C2[m, z + 1]
        return carry

    lax.fori_loop(0, macros, finish, 0)

    for gather in (gi, g0, g1, g2, g3):
        gather.drain()
    for copy, able in pending:
        @pl.when(able)
        def _(copy=copy):
            copy.wait_send()


def solution(mesh):
    n_dom, n_sub = mesh.shape["dom"], mesh.shape["sub"]
    side = 1
    while side * side * CORES < n_dom:
        side *= 2

    def local(source, zone_ids, kappa_table, mu_table, owner_dev, owner_group):
        macros, types, planes, cells = source.shape
        zones = kappa_table.shape[0]
        split = cells // 128
        src = source.reshape(macros, types, planes, split, 128)
        src = jnp.transpose(src, (0, 1, 3, 2, 4))
        zone = zone_ids.reshape(macros, split, 128)
        slots = owner_dev.shape[1]
        vmem = pl.BlockSpec(memory_space=pltpu.VMEM)
        smem = pl.BlockSpec(memory_space=pltpu.SMEM)

        def tiles(*lead):
            return pltpu.VMEM(lead + TILE, jnp.float32)

        m, rows = macros, n_dom + 1
        edge, pot = pl.pallas_call(
            functools.partial(kernel, side, n_sub, macros, zones),
            out_shape=(
                jax.ShapeDtypeStruct(src.shape, jnp.float32),
                jax.ShapeDtypeStruct((macros, split, planes, 128), jnp.float32),
            ),
            in_specs=[vmem, vmem, smem, vmem, vmem, smem, smem],
            out_specs=(vmem, vmem),
            scratch_shapes=[
                tiles(m, 7, 4), tiles(m, 7, 6), tiles(m, 7, 4),
                tiles(m, 7), tiles(m, 3), tiles(m, 7), tiles(m, 3),
                tiles(2, m, 4), tiles(m), tiles(2, m), tiles(m, 6), tiles(m, 6),
                tiles(m, 15), tiles(m, 7), tiles(m, 3), tiles(m, 3, 4), tiles(m), tiles(m), tiles(m, 4),
                tiles(rows, 5), tiles(rows, 1), tiles(rows, 3), tiles(rows, 1),
                pltpu.VMEM((n_dom,) + TILE, jnp.int32),
                tiles(4, 2), tiles(4, 2),
                pltpu.VMEM((128, 128), jnp.int32),
                pltpu.VMEM((slots, 128), jnp.int32),
                pltpu.VMEM((slots, 128), jnp.int32),
                pltpu.VMEM((slots, 128), jnp.int32),
                pltpu.SMEM((slots, 128), jnp.int32),
                pltpu.SemaphoreType.DMA((5, 3, 2, side)),
                pltpu.SemaphoreType.DMA((4, 2, 2)),
                pltpu.SemaphoreType.DMA((4, 2, 2)),
                pltpu.SemaphoreType.DMA,
            ],
            compiler_params=pltpu.CompilerParams(collective_id=0, has_side_effects=True),
        )(src, zone, owner_dev, owner_dev, owner_group, kappa_table.T, mu_table.T)

        def back(v):
            lead = v.shape[:-3]
            return jnp.swapaxes(v, -3, -2).reshape(lead + (planes, cells))

        return back(edge), back(pot)

    in_specs = (
        P("dom", None, "sub", None),
        P("dom", None),
        P(),
        P(),
        P("dom", None),
        P("dom", None),
    )
    out_specs = (P("dom", None, "sub", None), P("dom", "sub", None))
    return jax.shard_map(local, mesh=mesh, in_specs=in_specs, out_specs=out_specs, check_vma=False)
```

profile of v0, /device:TPU:1, one launch (start us, length us, event | category | flops | bytes accessed | tf_op | source)
XLA Modules:
  0.0 114.0 jit_solution(13384559781986550301)
XLA Ops:
  0.6 1.3 %copy.10 = s32[1,4,8,128]{3,2,1,0:T(8,128)} copy(s32[1,4,8,128]{3,1,2,0:T(4,128)} %bitcast.19) | data formatting | bytes 32768
  2.0 109.6 %shard_map.77 = (f32[4,7,8,4,128]{4,3,2,1,0:T(4,128)}, f32[4,8,4,128]{3,2,1,0:T(4,128)}) custom-call(f32[4,7,8,4,128]{4,3,2,1,0:T(4,128)} %bitcast.16, s32[4,8,128]{2,1,0:T(8,128)} %bitcast.17, s32[1,32]{1,0:T(1,128)} %od_v.1, s32[1,32]{1,0:T(1,128)} %od_v.1, s32[1,128]{1,0:T(1,128)} %og_v.1, f32[7,16]{1,0:T(8,128)} %bitcast.20, f32[8,16]{1,0:T(8,128)} %bitcast.21), custom_call_target="tpu_custom_call" | custom-call | tf_op jit(solution)/shard_map/pallas_call | solution.py:683
  111.5 0.0 copy-start
  111.5 1.8 %copy.13 = f32[4,7,4,1024]{3,2,1,0:T(4,128)} copy(f32[4,7,4,1024]{3,2,1,0:T(4,128)} %bitcast.15) | data formatting | bytes 917504
  113.4 0.0 copy-done
  113.4 0.6 copy.14
Async XLA Ops:
  111.5 1.9 %copy-start = (f32[4,8,4,128]{3,2,1,0:T(4,128)S(1)}, f32[4,8,4,128]{3,2,1,0:T(4,128)}, u32[]{:S(2)}) copy-start(f32[4,8,4,128]{3,2,1,0:T(4,128)} %get-tuple-element.5) | copy-start | bytes 196612
where the time goes:
time: 114 us
  Pallas kernels  110 us (96%)
  local copies, waits for them, and re-layouts  3.81 us (3%)
    pallas_call x1, Pallas kernels, local(): pl.pallas_call(functools.partial(kernel, side, n_sub, macros, zones), out...  110 us
    unnamed x5, local copies, waits for them, and re-layouts  3.81 us

commit v1 on v0

--- a/solution.py
+++ b/solution.py
@@ -24,7 +24,7 @@
     def __init__(self):
         self.lane = lax.broadcasted_iota(jnp.int32, TILE, 1)
         self.sub = lax.broadcasted_iota(jnp.int32, TILE, 0)
-        self.x = self.lane % LAT
+        self.x = self.lane & (LAT - 1)
         self.left = self.x == 0
         self.right = self.x == LAT - 1
         self.last_y = (self.sub == 7) & (self.lane >= 96)
@@ -50,10 +50,22 @@
         return jnp.where(self.first_y, 0.0, r)
 
     def pack(self, v, s, idx):
-        return pltpu.roll(jnp.where(self.side(s), v, 0.0), (idx - s * (LAT - 1) + 128) % 128, 1)
+        return pltpu.roll(jnp.where(self.side(s), v, jnp.zeros_like(v)), (idx - s * (LAT - 1)) & 127, 1)
 
     def unpack(self, v, s, idx):
-        return pltpu.roll(v, (s * (LAT - 1) - idx + 128) % 128, 1)
+        return pltpu.roll(v, (s * (LAT - 1) - idx) & 127, 1)
+
+
+def near_first(side):
+    return sorted(range(1, side), key=lambda i: min(i, side - i))
+
+
+def run_second(gathers):
+    for i in [0] + near_first(gathers[0].side):
+        for gather in gathers:
+            gather.step(i)
+    for gather in gathers:
+        gather.second_done()
 
 
 class Gather:
@@ -69,8 +81,8 @@
     def line(self, core, a):
         return self.buf.at[pl.ds((core * self.side + a) * self.side, self.side)]
 
-    def send(self, stage, i, ref, target):
-        copy = pltpu.make_async_remote_copy(
+    def copy(self, stage, i, ref, target):
+        return pltpu.make_async_remote_copy(
             src_ref=ref,
             dst_ref=ref,
             send_sem=self.sems.at[stage, 0, i],
@@ -78,35 +90,42 @@
             device_id=target,
             device_id_type=MESH,
         )
+
+    def send(self, stage, i, ref, target):
+        copy = self.copy(stage, i, ref, target)
         copy.start()
         self.sent.append(copy)
 
     def arrived(self, stage, i, ref):
-        pltpu.make_async_remote_copy(
-            src_ref=ref,
-            dst_ref=ref,
-            send_sem=self.sems.at[stage, 0, i],
-            recv_sem=self.sems.at[stage, 1, i],
-            device_id=self.dev(self.core, self.a, self.b),
-            device_id_type=MESH,
-        ).wait_recv()
+        self.copy(stage, i, ref, self.dev(self.core, self.a, self.b)).wait_recv()
 
     def first(self):
         ref = self.buf.at[self.row()]
         for i in range(1, self.side):
             self.send(0, i, ref, self.dev(self.core, self.a, (self.b + i) % self.side))
 
-    def second(self):
+    def forward(self, row):
+        ref = self.buf.at[row]
         for i in range(1, self.side):
-            source = (self.b - i + self.side) % self.side
-            self.arrived(0, i, self.buf.at[(self.core * self.side + self.a) * self.side + source])
+            self.copy(1, i, ref, self.dev(self.core, (self.a + i) % self.side, self.b)).start()
+
+    def step(self, i):
+        row = (self.core * self.side + self.a) * self.side + (self.b - i + self.side) % self.side
+        if i:
+            self.arrived(0, i, self.buf.at[row])
+        self.forward(row)
+
+    def second_done(self):
         ref = self.line(self.core, self.a)
         for i in range(1, self.side):
-            self.send(1, i, ref, self.dev(self.core, (self.a + i) % self.side, self.b))
+            self.sent.append(self.copy(1, i, ref, self.dev(self.core, self.a, self.b)))
         self.send(2, 0, ref, self.dev(1 - self.core, self.b, self.a))
 
+    def second(self):
+        run_second([self])
+
     def third(self):
-        for i in range(1, self.side):
+        for i in near_first(self.side):
             ref = self.line(self.core, (self.a - i + self.side) % self.side)
             self.arrived(1, i, ref)
             self.send(2, i, ref, self.dev(1 - self.core, self.b, self.a))
@@ -125,10 +144,10 @@
     src, zone, od_s, od_v, og_v, kappa, mu,
     out_e, out_p,
     S, EF, R, SB, SA, RB, RA, NR, NB, NA, C1, C2,
-    MC, INVH, INV0, INVS, NDH, ND0, ND,
+    MC, INVH, INV0, INVS, NDH, DIAG, DSUM, ZS, ND,
     G0, G1, G2, G3, GI, HS, HR,
-    ODS, GRS, JS, IDXV, IDXS,
-    gsem, bsem, hsem, isem,
+    SRC, ODS, OD2, GRS, JS, IDXV, IDXS,
+    gsem, bsem, hsem, isem, lsem,
 ):
     dom = lax.axis_index("dom")
     k = lax.axis_index("sub")
@@ -164,6 +183,8 @@
     def _():
         greet((dom, k - 1))
 
+    load = pltpu.make_async_copy(src, SRC, lsem)
+    load.start()
     ln = Lanes()
     ahead = {0: ln.ax, 1: ln.ay, 3: lambda v: ln.ax(ln.ay(v))}
     behind = {0: ln.bx, 1: ln.by, 3: lambda v: ln.bx(ln.by(v))}
@@ -182,26 +203,51 @@
     g3 = Gather(G3, gsem.at[3], me, side)
     row = gi.row()
 
-    GI[row] = jnp.full(TILE, -1, jnp.int32)
-    GI[row, 0:1, 0 : og_v.shape[1]] = og_v[...]
-    GI[row, 1:2, 0 : od_v.shape[1]] = od_v[...]
-
-    def prepare(m, packs):
-        zid = zone[m]
-        hits = [zid == zz for zz in range(zones)]
-        mass, curl = [], []
+    GI[nd_dev] = jnp.full(TILE, zones, jnp.int32)
+    IDXV[0:1, 0 : og_v.shape[1]] = og_v[...]
+    IDXV[1:2, :] = jnp.full((1, 128), -1, jnp.int32)
+    IDXV[1:2, 0 : od_v.shape[1]] = od_v[...]
+    upper = lax.broadcasted_iota(jnp.int32, (1, 128), 1) & 31 >= 16
+    zone_pack = jnp.zeros(TILE, jnp.int32)
+    for m in range(macros):
+        zid = zone[:, m, :]
+        ZS[m] = zid
+        zone_pack = zone_pack + ln.pack(zid, 0, m * 4) + ln.pack(jnp.full(TILE, zones, jnp.int32), 0, m * 4 + 1)
+        zone_pack = zone_pack + ln.pack(zid, 1, m * 4 + 2) + ln.pack(pltpu.roll(zid, 1, 1), 1, m * 4 + 3)
+    GI[row] = zone_pack
+    for n in range(2):
+        v = IDXV[n : n + 1, :]
+        GI[row, 2 * n : 2 * n + 1, :] = jnp.where(upper, pltpu.roll(v, 16, 1), zone_pack[2 * n : 2 * n + 1])
+        GI[row, 2 * n + 1 : 2 * n + 2, :] = jnp.where(upper, v, zone_pack[2 * n + 1 : 2 * n + 2])
+
+    def load_source(m, packs):
+        packs = list(packs)
         for t in range(7):
-            v = zero
-            for zz in range(zones):
-                v = jnp.where(hits[zz], kappa[t, zz], v)
-            mass.append(v)
-            MC[m, t] = v
+            for p in range(PLANES):
+                v = SRC[m, t, :, p, :]
+                S[m, POS[t], p] = v
+                if t in SHARED:
+                    n = SHARED.index(t)
+                    for s in range(2):
+                        packs[n] = packs[n] + ln.pack(v, s, (m * 2 + s) * 4 + p)
+        return tuple(packs)
+
+    load.wait()
+    packs = lax.fori_loop(0, macros, load_source, (zero,) * 3)
+    for u in range(3):
+        G0[row, u] = packs[u]
+
+    def prepare(m, carry):
+        zid = ZS[m]
+        mass, curl = [zero] * 7, [zero] * 8
+        for zz in range(zones):
+            hit = zid == zz
+            mass = [jnp.where(hit, kappa[t, zz], v) for t, v in enumerate(mass)]
+            curl = [jnp.where(hit, mu[f, zz], v) for f, v in enumerate(curl)]
+        for t in range(7):
+            MC[m, t] = mass[t]
         for f in range(8):
-            v = zero
-            for zz in range(zones):
-                v = jnp.where(hits[zz], mu[f, zz], v)
-            curl.append(v)
-            MC[m, 7 + f] = v
+            MC[m, 7 + f] = curl[f]
         diag = {
             0: mass[0] + curl[0] + curl[2] + behind[1](curl[1]),
             1: mass[1] + curl[1] + curl[4] + behind[0](curl[0]),
@@ -220,31 +266,14 @@
             INVH[m, POS[t]] = EDGE_DAMPING / full[t]
         for n, t in enumerate(FLAT_TYPES):
             INV0[m, n] = EDGE_DAMPING / first[t]
-        for n, t in enumerate(SHARED):
-            INVS[m, n, 0] = first[t]
-            for p in range(1, PLANES):
-                INVS[m, n, p] = full[t]
         node_full, node_first = node + node_low, node + inside0 * node_low
         NDH[m] = NODE_DAMPING / node_full
-        ND[m, 0] = node_first
-        for p in range(1, PLANES):
-            ND[m, p] = node_full
-        for t in range(7):
-            for p in range(PLANES):
-                S[m, POS[t], p] = src[m, t, :, p, :]
-        packs = list(packs)
-        for s in range(2):
-            for n, t in enumerate(SHARED):
-                for p in range(PLANES):
-                    packs[n] = packs[n] + ln.pack(S[m, POS[t], p], s, (m * 2 + s) * 4 + p)
-            for n, (f_, g_) in enumerate([(full[t], first[t]) for t in SHARED] + [(node_full, node_first)]):
-                packs[3] = packs[3] + ln.pack(f_, s, (m * 2 + s) * 4 + n)
-                packs[4] = packs[4] + ln.pack(g_, s, (m * 2 + s) * 4 + n)
-        return tuple(packs)
-
-    packs = lax.fori_loop(0, macros, prepare, (zero,) * 5)
-    for u in range(5):
-        G0[row, u] = packs[u]
+        for n, t in enumerate(SHARED):
+            DIAG[m, 0, n] = first[t]
+            DIAG[m, 1, n] = full[t]
+        DIAG[m, 0, 3] = node_first
+        DIAG[m, 1, 3] = node_full
+        return carry
 
     pl.semaphore_wait(
         barrier, 2 * (side - 1) + 1 + jnp.where(has_up, 1, 0) + jnp.where(has_down, 1, 0)
@@ -315,44 +344,48 @@
                 EF[m, POS[t], p + 1] = inverse(m, t, p) * S[m, POS[t], p]
         return carry
 
+    lax.fori_loop(0, macros, prepare, 0)
     lax.fori_loop(0, macros, start_private, 0)
-    gi.second()
-    g0.second()
+    run_second([gi])
+    run_second([g0])
     gi.third()
     gi.finish()
 
-    def place(r, carry):
-        c_ = r // (side * side)
-        a_ = (r // side) % side
-        b_ = r % side
-        natural = jnp.where(c_ == 0, a_ * side + b_, b_ * side + a_) * CORES + c_
-        ODS[pl.ds(natural, 1), :] = GI[r, 1:2, :]
-        return carry
+    slots = od_v.shape[1]
+    bits = side.bit_length() - 1
+
+    def row_of(device):
+        c_ = device & (CORES - 1)
+        z_ = device >> (1 + bits)
+        y_ = (device >> 1) & (side - 1)
+        return (c_ << (2 * bits)) + jnp.where(c_ == 0, (z_ << bits) + y_, (y_ << bits) + z_)
 
     ODS[...] = jnp.full(ODS.shape, -1, jnp.int32)
-    lax.fori_loop(0, nd_dev, place, 0)
-    slots = od_v.shape[1]
+    OD2[...] = jnp.full(ODS.shape, -1, jnp.int32)
+    for device in range(nd_dev):
+        c_, z_, y_ = device % CORES, device // (CORES * side), device // CORES % side
+        r = c_ * side * side + (y_ * side + z_ if c_ else z_ * side + y_)
+        ODS[device : device + 1, :] = GI[r, 2:3, :]
+        OD2[device : device + 1, :] = GI[r, 3:4, :]
+    upper_all = lax.broadcasted_iota(jnp.int32, ODS.shape, 1) & 31 >= 16
+    ODS[...] = jnp.where(upper_all, OD2[...], pltpu.roll(ODS[...], 112, 1))
     owners = jnp.transpose(ODS[...])[0:slots]
     number = lax.broadcasted_iota(jnp.int32, owners.shape, 0) + 1
 
-    def look(j, carry):
-        e = od_s[0, j]
-        c_ = e % CORES
-        z_ = e // (CORES * side)
-        y_ = (e // CORES) % side
-        r = c_ * side * side + jnp.where(c_ == 0, z_ * side + y_, y_ * side + z_)
-        GRS[pl.ds(j, 1), :] = GI[r, 0:1, :]
-        hit = jnp.where(owners == e, number, 0)
-        JS[pl.ds(j, 1), :] = jnp.max(hit, axis=0, keepdims=True)
+    def look(block, carry):
+        for jj in range(8):
+            j = block * 8 + jj
+            e = od_s[0, j]
+            two = GI[row_of(e), 0:2, :]
+            GRS[pl.ds(j, 1), :] = jnp.where(upper, two[1:2], pltpu.roll(two[0:1], 112, 1))
+            JS[pl.ds(j, 1), :] = jnp.max(jnp.where(owners == e, number, 0), axis=0, keepdims=True)
         return carry
 
-    lax.fori_loop(0, slots, look, 0)
+    lax.fori_loop(0, slots // 8, look, 0)
     group, place_of = GRS[...], JS[...]
     device = lax.broadcasted_iota(jnp.int32, group.shape, 1)
-    c_ = device % CORES
-    z_ = device // (CORES * side)
-    y_ = (device // CORES) % side
-    rows = (c_ * side * side + jnp.where(c_ == 0, z_ * side + y_, y_ * side + z_))
+    slot = lax.broadcasted_iota(jnp.int32, group.shape, 0)
+    rows = row_of(device)
     mine = jnp.max(jnp.where(device == dom, group, -2), axis=1, keepdims=True)
     mate = (group == mine) & (place_of > 0) & (device != dom)
     none = nd_dev * 32
@@ -360,12 +393,71 @@
     found = jnp.zeros(group.shape, jnp.int32)
     for i in range(3):
         least = jnp.min(code, axis=1, keepdims=True)
-        found = jnp.where(device == i, least, found)
+        theirs = least & 31
+        low = theirs & 3
+        found = jnp.where(device == i, jnp.clip(least >> 5, 0, nd_dev), found)
+        found = jnp.where(device == 4 + i, (((slot >> 2) & 1) * (LAT - 1) - theirs) & 127, found)
+        found = jnp.where(device == 8 + i, (slot - (theirs >> 2) * 2) & 127, found)
+        found = jnp.where(device == 12 + i, low, found)
         code = jnp.where(code == least, none, code)
-    IDXV[...] = jnp.clip(found, 0, none)
+    IDXV[...] = found
     to_scalar = pltpu.make_async_copy(IDXV, IDXS, isem)
     to_scalar.start()
     to_scalar.wait()
+
+    def mate_row(j, i):
+        return jnp.clip(IDXS[j, i], 0, nd_dev)
+
+    def fetch(block, carry):
+        own, left, inner = [list(c) for c in carry]
+        for jj in range(4):
+            j = block * 4 + jj
+            here = ln.x == j
+            for i in range(3):
+                v = GI[mate_row(j, i)]
+                turn = IDXS[j, 8 + i]
+                own[i] = jnp.where(here, pltpu.roll(v, turn, 1), own[i])
+                left[i] = jnp.where(here, pltpu.roll(v, (turn - 1) & 127, 1), left[i])
+                inner[i] = jnp.where(here, jnp.where(IDXS[j, 12 + i] == 0, inside0, 1.0), inner[i])
+        return tuple(own), tuple(left), tuple(inner)
+
+    izero = jnp.full(TILE, zones, jnp.int32)
+    own, left, inner = lax.fori_loop(0, slots // 4, fetch, ((izero,) * 3, (izero,) * 3, (zero,) * 3))
+    sums = [zero] * 4
+    for i in range(3):
+        mass = {t: zero for t in range(7)}
+        curl = {f: zero for f in (1, 3, 4, 5, 7)}
+        mass_x = {t: zero for t in (0, 3, 4, 6)}
+        curl_x = {f: zero for f in (0, 2, 6)}
+        for zz in range(zones):
+            hit, hit_x = own[i] == zz, left[i] == zz
+            mass = {t: jnp.where(hit, kappa[t, zz], v) for t, v in mass.items()}
+            curl = {f: jnp.where(hit, mu[f, zz], v) for f, v in curl.items()}
+            mass_x = {t: jnp.where(hit_x, kappa[t, zz], v) for t, v in mass_x.items()}
+            curl_x = {f: jnp.where(hit_x, mu[f, zz], v) for f, v in curl_x.items()}
+        sums[0] = sums[0] + mass[1] + curl[1] + curl[4] + curl_x[0] + inner[i] * curl[5]
+        sums[1] = sums[1] + mass[2] + curl[3] + curl[5] + curl[7] + curl_x[2] + ln.by(curl[4] + curl_x[6])
+        sums[2] = sums[2] + mass[5] + curl[4] + curl[5]
+        sums[3] = sums[3] + functools.reduce(lambda p, q: p + q, [mass[t] for t in range(7)]) + mass_x[0]
+        sums[3] = sums[3] + ln.by(mass[1] + mass_x[3])
+        sums[3] = sums[3] + inner[i] * (mass[2] + mass_x[4] + ln.by(mass[5] + mass_x[6]))
+    for n in range(4):
+        DSUM[n] = sums[n]
+
+    def invert(m, carry):
+        for n in range(4):
+            extra = DSUM[n]
+            for p in range(PLANES):
+                v = DIAG[m, 1 if p else 0, n]
+                for s in range(2):
+                    v = jnp.where(ln.side(s), v + ln.unpack(extra, s, (m * 2 + s) * 4 + p), v)
+                if n < 3:
+                    INVS[m, n, p] = EDGE_DAMPING / v
+                else:
+                    ND[m, p] = NODE_DAMPING / v
+        return carry
+
+    lax.fori_loop(0, macros, invert, 0)
 
     g0.third()
     g0.finish()
@@ -374,25 +466,9 @@
         j = (m * 2 + s) * 4 + p
         totals = [None] * len(units)
         for i in range(3):
-            code = IDXS[j, i]
-            r = jnp.clip(code // 32, 0, nd_dev)
-            theirs = code % 32
+            r, turn = mate_row(j, i), IDXS[j, 4 + i]
             for n, u in enumerate(units):
-                v = ln.unpack(buf[r, u], s, theirs)
-                totals[n] = v if totals[n] is None else totals[n] + v
-        return totals
-
-    def others_diag(m, p, s):
-        j = (m * 2 + s) * 4 + p
-        totals = [None] * 4
-        for i in range(3):
-            code = IDXS[j, i]
-            r = jnp.clip(code // 32, 0, nd_dev)
-            theirs = code % 32
-            low = theirs % 4
-            v0 = G0[r, jnp.where(low == 0, 4, 3)]
-            for n in range(4):
-                v = ln.unpack(v0, s, theirs - low + n)
+                v = pltpu.roll(buf[r, u], turn, 1)
                 totals[n] = v if totals[n] is None else totals[n] + v
         return totals
 
@@ -406,15 +482,8 @@
         up, down = carry
         for p in range(PLANES):
             values = assembled(G0, (0, 1, 2), m, p, [S[m, POS[t], p] for t in SHARED])
-            diags = [INVS[m, n, p] for n in range(3)] + [ND[m, p]]
-            for s in range(2):
-                extra = others_diag(m, p, s)
-                diags = [jnp.where(ln.side(s), v + e, v) for v, e in zip(diags, extra)]
-            ND[m, p] = NODE_DAMPING / diags[3]
             for n, t in enumerate(SHARED):
-                inv = EDGE_DAMPING / diags[n]
-                INVS[m, n, p] = inv
-                new = inv * values[n]
+                new = INVS[m, n, p] * values[n]
                 EF[m, POS[t], p + 1] = new
                 for s in range(2):
                     if p == PLANES - 1:
@@ -671,7 +740,7 @@
         split = cells // 128
         src = source.reshape(macros, types, planes, split, 128)
         src = jnp.transpose(src, (0, 1, 3, 2, 4))
-        zone = zone_ids.reshape(macros, split, 128)
+        zone = jnp.transpose(zone_ids.reshape(macros, split, 128), (1, 0, 2))
         slots = owner_dev.shape[1]
         vmem = pl.BlockSpec(memory_space=pltpu.VMEM)
         smem = pl.BlockSpec(memory_space=pltpu.SMEM)
@@ -686,16 +755,19 @@
                 jax.ShapeDtypeStruct(src.shape, jnp.float32),
                 jax.ShapeDtypeStruct((macros, split, planes, 128), jnp.float32),
             ),
-            in_specs=[vmem, vmem, smem, vmem, vmem, smem, smem],
+            in_specs=[pl.BlockSpec(memory_space=pl.ANY), vmem, smem, vmem, vmem, smem, smem],
             out_specs=(vmem, vmem),
             scratch_shapes=[
                 tiles(m, 7, 4), tiles(m, 7, 6), tiles(m, 7, 4),
                 tiles(m, 7), tiles(m, 3), tiles(m, 7), tiles(m, 3),
                 tiles(2, m, 4), tiles(m), tiles(2, m), tiles(m, 6), tiles(m, 6),
-                tiles(m, 15), tiles(m, 7), tiles(m, 3), tiles(m, 3, 4), tiles(m), tiles(m), tiles(m, 4),
-                tiles(rows, 5), tiles(rows, 1), tiles(rows, 3), tiles(rows, 1),
-                pltpu.VMEM((n_dom,) + TILE, jnp.int32),
+                tiles(m, 15), tiles(m, 7), tiles(m, 3), tiles(m, 3, 4), tiles(m), tiles(m, 2, 4), tiles(4),
+                pltpu.VMEM((m,) + TILE, jnp.int32), tiles(m, 4),
+                tiles(rows, 3), tiles(rows, 1), tiles(rows, 3), tiles(rows, 1),
+                pltpu.VMEM((rows,) + TILE, jnp.int32),
                 tiles(4, 2), tiles(4, 2),
+                pltpu.VMEM((macros, types, split, planes, 128), jnp.float32),
+                pltpu.VMEM((128, 128), jnp.int32),
                 pltpu.VMEM((128, 128), jnp.int32),
                 pltpu.VMEM((slots, 128), jnp.int32),
                 pltpu.VMEM((slots, 128), jnp.int32),
@@ -704,6 +776,7 @@
                 pltpu.SemaphoreType.DMA((5, 3, 2, side)),
                 pltpu.SemaphoreType.DMA((4, 2, 2)),
                 pltpu.SemaphoreType.DMA((4, 2, 2)),
+                pltpu.SemaphoreType.DMA,
                 pltpu.SemaphoreType.DMA,
             ],
             compiler_params=pltpu.CompilerParams(collective_id=0, has_side_effects=True),

time: 114 us -> 97.4 us (0.85)
  Pallas kernels: 110 us -> 94 us
  local copies, waits for them, and re-layouts: 3.81 us -> 2.48 us
    pallas_call x1, Pallas kernels: 110 us -> 94 us  [local(): pl.pallas_call(functools.partial(kernel, side, n_sub, macros, zones), out...]
    unnamed x5 -> x4, local copies, waits for them, and re-layouts: 3.81 us -> 2.48 us
where the time goes in v1:
time: 97.4 us; the launch traced here: 97.1 us
  Pallas kernels  94 us (97%)
  local copies, waits for them, and re-layouts  2.48 us (3%)
    pallas_call x1, Pallas kernels, local(): pl.pallas_call(functools.partial(kernel, side, n_sub, macros, zones), out...  94 us
    unnamed x4, local copies, waits for them, and re-layouts  2.48 us

profile of v1, /device:TPU:1, one launch (start us, length us, event | category | flops | bytes accessed | tf_op | source)
XLA Modules:
  0.0 97.1 jit_solution(9610220671956736007)
XLA Ops:
  0.6 94.0 %shard_map.77 = (f32[4,7,8,4,128]{4,3,2,1,0:T(4,128)}, f32[4,8,4,128]{3,2,1,0:T(4,128)}) custom-call(f32[4,7,8,4,128]{4,3,2,1,0:T(4,128)} %bitcast.15, s32[8,4,128]{2,1,0:T(4,128)} %bitcast.17, s32[1,32]{1,0:T(1,128)} %od_v.1, s32[1,32]{1,0:T(1,128)} %od_v.1, s32[1,128]{1,0:T(1,128)} %og_v.1, f32[7,16]{1,0:T(8,128)} %bitcast.18, f32[8,16]{1,0:T(8,128)} %bitcast.19), custom_call_target="tpu_custom_call" | custom-call | tf_op jit(solution)/shard_map/pallas_call | solution.py:752
  94.6 0.0 copy-start
  94.6 1.8 %copy.10 = f32[4,7,4,1024]{3,2,1,0:T(4,128)} copy(f32[4,7,4,1024]{3,2,1,0:T(4,128)} %bitcast.14) | data formatting | bytes 917504
  96.5 0.0 copy-done
  96.5 0.6 copy.11
Async XLA Ops:
  94.6 1.9 %copy-start = (f32[4,8,4,128]{3,2,1,0:T(4,128)S(1)}, f32[4,8,4,128]{3,2,1,0:T(4,128)}, u32[]{:S(2)}) copy-start(f32[4,8,4,128]{3,2,1,0:T(4,128)} %get-tuple-element.5) | copy-start | bytes 196612

commit v2 on v1

--- a/solution.py
+++ b/solution.py
@@ -60,11 +60,14 @@
     return sorted(range(1, side), key=lambda i: min(i, side - i))
 
 
-def run_second(gathers):
-    for i in [0] + near_first(gathers[0].side):
+def run_second(gathers, together=0):
+    order = near_first(gathers[0].side)
+    for i in order[:together]:
         for gather in gathers:
             gather.step(i)
     for gather in gathers:
+        for i in order[together:]:
+            gather.step(i)
         gather.second_done()
 
 
@@ -122,6 +125,7 @@
         self.send(2, 0, ref, self.dev(1 - self.core, self.b, self.a))
 
     def second(self):
+        self.step(0)
         run_second([self])
 
     def third(self):
@@ -144,7 +148,7 @@
     src, zone, od_s, od_v, og_v, kappa, mu,
     out_e, out_p,
     S, EF, R, SB, SA, RB, RA, NR, NB, NA, C1, C2,
-    MC, INVH, INV0, INVS, NDH, DIAG, DSUM, ZS, ND,
+    MC, INVH, INV0, INVP, NDH, ND0, EP, ZS,
     G0, G1, G2, G3, GI, HS, HR,
     SRC, ODS, OD2, GRS, JS, IDXV, IDXS,
     gsem, bsem, hsem, isem, lsem,
@@ -237,7 +241,7 @@
     for u in range(3):
         G0[row, u] = packs[u]
 
-    def prepare(m, carry):
+    def prepare(m, packs):
         zid = ZS[m]
         mass, curl = [zero] * 7, [zero] * 8
         for zz in range(zones):
@@ -268,12 +272,13 @@
             INV0[m, n] = EDGE_DAMPING / first[t]
         node_full, node_first = node + node_low, node + inside0 * node_low
         NDH[m] = NODE_DAMPING / node_full
-        for n, t in enumerate(SHARED):
-            DIAG[m, 0, n] = first[t]
-            DIAG[m, 1, n] = full[t]
-        DIAG[m, 0, 3] = node_first
-        DIAG[m, 1, 3] = node_full
-        return carry
+        ND0[m] = NODE_DAMPING / node_first
+        packs = list(packs)
+        for n, (f_, g_) in enumerate([(full[t], first[t]) for t in SHARED] + [(node_full, node_first)]):
+            for s in range(2):
+                for p in range(PLANES):
+                    packs[n] = packs[n] + ln.pack(f_ if p else g_, s, (m * 2 + s) * 4 + p)
+        return tuple(packs)
 
     pl.semaphore_wait(
         barrier, 2 * (side - 1) + 1 + jnp.where(has_up, 1, 0) + jnp.where(has_down, 1, 0)
@@ -318,7 +323,8 @@
         RB[...] = jnp.zeros_like(RB)
         NB[...] = jnp.zeros_like(NB)
         for i in range(4):
-            HR[i, 0] = zero
+            for n in range(3):
+                HR[i, 0, n] = zero
 
     @pl.when(jnp.logical_not(has_up))
     def _():
@@ -326,7 +332,8 @@
         RA[...] = jnp.zeros_like(RA)
         NA[...] = jnp.zeros_like(NA)
         for i in range(4):
-            HR[i, 1] = zero
+            for n in range(3):
+                HR[i, 1, n] = zero
 
     s_up = (0, S.at[:, :, PLANES - 1], SB, bsem, 0)
     s_down = (1, S.at[:, 0:3, 0], SA, bsem, 0)
@@ -338,16 +345,34 @@
             return INV0[m, POS[t]]
         return INVH[m, POS[t]]
 
-    def start_private(m, carry):
-        for t in PRIVATE:
+    def halo_edges(below, above, fresh):
+        def body(m, carry):
+            for t in range(7):
+                v = INVH[m, POS[t]] * below[m, POS[t]]
+                EF[m, POS[t], 0] = v if fresh else EF[m, POS[t], 0] + v
+            for t in FLAT_TYPES:
+                v = INVH[m, POS[t]] * above[m, POS[t]]
+                EF[m, POS[t], PLANES + 1] = v if fresh else EF[m, POS[t], PLANES + 1] + v
+            return carry
+
+        lax.fori_loop(0, macros, body, 0)
+
+    def start_all(m, carry):
+        for t in range(7):
             for p in range(PLANES):
                 EF[m, POS[t], p + 1] = inverse(m, t, p) * S[m, POS[t], p]
         return carry
 
-    lax.fori_loop(0, macros, prepare, 0)
-    lax.fori_loop(0, macros, start_private, 0)
-    run_second([gi])
-    run_second([g0])
+    gi.step(0)
+    g0.step(0)
+    diag_sides = lax.fori_loop(0, macros, prepare, (zero,) * 4)
+    for n in range(4):
+        INVP[n] = diag_sides[n]
+    run_second([gi, g0], 0)
+    lax.fori_loop(0, macros, start_all, 0)
+    pull(*s_up)
+    pull(*s_down)
+    halo_edges(SB, SA, True)
     gi.third()
     gi.finish()
 
@@ -396,7 +421,7 @@
         theirs = least & 31
         low = theirs & 3
         found = jnp.where(device == i, jnp.clip(least >> 5, 0, nd_dev), found)
-        found = jnp.where(device == 4 + i, (((slot >> 2) & 1) * (LAT - 1) - theirs) & 127, found)
+        found = jnp.where(device == 4 + i, (slot - theirs) & 127, found)
         found = jnp.where(device == 8 + i, (slot - (theirs >> 2) * 2) & 127, found)
         found = jnp.where(device == 12 + i, low, found)
         code = jnp.where(code == least, none, code)
@@ -442,101 +467,66 @@
         sums[3] = sums[3] + ln.by(mass[1] + mass_x[3])
         sums[3] = sums[3] + inner[i] * (mass[2] + mass_x[4] + ln.by(mass[5] + mass_x[6]))
     for n in range(4):
-        DSUM[n] = sums[n]
-
-    def invert(m, carry):
-        for n in range(4):
-            extra = DSUM[n]
-            for p in range(PLANES):
-                v = DIAG[m, 1 if p else 0, n]
-                for s in range(2):
-                    v = jnp.where(ln.side(s), v + ln.unpack(extra, s, (m * 2 + s) * 4 + p), v)
-                if n < 3:
-                    INVS[m, n, p] = EDGE_DAMPING / v
-                else:
-                    ND[m, p] = NODE_DAMPING / v
-        return carry
-
-    lax.fori_loop(0, macros, invert, 0)
+        INVP[n] = (EDGE_DAMPING if n < 3 else NODE_DAMPING) / (INVP[n] + sums[n])
 
     g0.third()
     g0.finish()
 
-    def others(buf, units, m, p, s):
-        j = (m * 2 + s) * 4 + p
-        totals = [None] * len(units)
-        for i in range(3):
-            r, turn = mate_row(j, i), IDXS[j, 4 + i]
-            for n, u in enumerate(units):
-                v = pltpu.roll(buf[r, u], turn, 1)
-                totals[n] = v if totals[n] is None else totals[n] + v
-        return totals
-
-    def assembled(buf, units, m, p, values):
+    def mates(buf, units):
+        def body(m, acc):
+            acc = list(acc)
+            for q in range(8):
+                j = m * 8 + q
+                here = ln.x == j
+                totals = [None] * len(units)
+                for i in range(3):
+                    r, turn = mate_row(j, i), IDXS[j, 4 + i]
+                    for n, u in enumerate(units):
+                        v = pltpu.roll(buf[r, u], turn, 1)
+                        totals[n] = v if totals[n] is None else totals[n] + v
+                acc = [jnp.where(here, t, v) for t, v in zip(totals, acc)]
+            return tuple(acc)
+
+        return lax.fori_loop(0, macros, body, (zero,) * len(units))
+
+    def sides_message(event, edges):
+        last = 3 if edges else 1
+        up_ = (0, HS.at[event, 0:last], HR.at[event, 0, 0:last], hsem, event)
+        down_ = (1, HS.at[event, 0:1], HR.at[event, 1, 0:1], hsem, event)
+        return up_, down_
+
+    def replace(v, packed, m, p):
         for s in range(2):
-            extra = others(buf, units, m, p, s)
-            values = [jnp.where(ln.side(s), v + e, v) for v, e in zip(values, extra)]
-        return values
-
-    def start_shared(m, carry):
-        up, down = carry
-        for p in range(PLANES):
-            values = assembled(G0, (0, 1, 2), m, p, [S[m, POS[t], p] for t in SHARED])
+            v = jnp.where(ln.side(s), ln.unpack(packed, s, (m * 2 + s) * 4 + p), v)
+        return v
+
+    def edge_sides(event, values):
+        for n in range(3):
+            HS[event, n] = values[n]
+        up_, down_ = sides_message(event, True)
+        push(*up_)
+        push(*down_)
+
+        def own(m, carry):
             for n, t in enumerate(SHARED):
-                new = INVS[m, n, p] * values[n]
-                EF[m, POS[t], p + 1] = new
-                for s in range(2):
-                    if p == PLANES - 1:
-                        up = up + ln.pack(new, s, (m * 2 + s) * 4 + n)
-                    if p == 0 and t == 1:
-                        down = down + ln.pack(new, s, (m * 2 + s) * 4 + n)
-        return up, down
-
-    def send_sides(event, up, down, both=True):
-        if both:
-            HS[event, 0] = up
-            push(0, HS.at[event, 0], HR.at[event, 0], hsem, event)
-        HS[event, 1] = down
-        push(1, HS.at[event, 1], HR.at[event, 1], hsem, event)
-
-    def take_sides(event, both=True):
-        if both:
-            pull(0, HS.at[event, 0], HR.at[event, 0], hsem, event)
-        pull(1, HS.at[event, 1], HR.at[event, 1], hsem, event)
-
-    def replace(v, packed, m, n):
-        for s in range(2):
-            v = jnp.where(ln.side(s), ln.unpack(packed, s, (m * 2 + s) * 4 + n), v)
-        return v
-
-    up, down = lax.fori_loop(0, macros, start_shared, (zero, zero))
-    send_sides(0, up, down)
-    pull(*s_up)
-    pull(*s_down)
-    take_sides(0)
-
-    def halo_edges(event, below, above, fresh):
-        def body(m, carry):
-            from_below, from_above = HR[event, 0], HR[event, 1]
-            for t in range(7):
-                v = INVH[m, POS[t]] * below[m, POS[t]]
-                if not fresh:
-                    v = EF[m, POS[t], 0] + v
-                if t in SHARED:
-                    v = replace(v, from_below, m, SHARED.index(t))
-                EF[m, POS[t], 0] = v
-            for t in FLAT_TYPES:
-                v = INVH[m, POS[t]] * above[m, POS[t]]
-                if not fresh:
-                    v = EF[m, POS[t], PLANES + 1] + v
-                if t in SHARED:
-                    v = replace(v, from_above, m, 0)
-                EF[m, POS[t], PLANES + 1] = v
+                for p in range(PLANES):
+                    EF[m, POS[t], p + 1] = replace(EF[m, POS[t], p + 1], HS[event, n], m, p)
             return carry
 
-        lax.fori_loop(0, macros, body, 0)
-
-    halo_edges(0, SB, SA, True)
+        lax.fori_loop(0, macros, own, 0)
+        pull(*up_)
+        pull(*down_)
+
+        def halo(m, carry):
+            for n, t in enumerate(SHARED):
+                EF[m, POS[t], 0] = replace(EF[m, POS[t], 0], HR[event, 0, n], m, PLANES - 1)
+            EF[m, POS[1], PLANES + 1] = replace(EF[m, POS[1], PLANES + 1], HR[event, 1, 0], m, 0)
+            return carry
+
+        lax.fori_loop(0, macros, halo, 0)
+
+    extra = mates(G0, (0, 1, 2))
+    edge_sides(0, [INVP[n] * (G0[row, n] + extra[n]) for n in range(3)])
 
     def operate(m, want_nodes, sink):
         mass = [MC[m, t] for t in range(7)]
@@ -601,38 +591,52 @@
         if both:
             push(*n_up)
         push(*n_down)
+
+        def interior(m, carry):
+            for p in range(PLANES):
+                corr[m, p + 1] = (NDH[m] if p else ND0[m]) * NR[sweep, m, p]
+            return carry
+
         gather.second()
-        gather.third()
-        gather.finish()
-
-        def correct(m, carry):
-            up_, down_ = carry
-            for p in range(PLANES):
-                (value,) = assembled(buf, (0,), m, p, [NR[sweep, m, p]])
-                value = ND[m, p] * value
-                corr[m, p + 1] = value
-                for s in range(2):
-                    if p == PLANES - 1:
-                        up_ = up_ + ln.pack(value, s, (m * 2 + s) * 4)
-                    if p == 0:
-                        down_ = down_ + ln.pack(value, s, (m * 2 + s) * 4)
-            return up_, down_
-
-        up_, down_ = lax.fori_loop(0, macros, correct, (zero, zero))
-        event = 1 + 2 * sweep
-        send_sides(event, up_, down_, both)
+        lax.fori_loop(0, macros, interior, 0)
         if both:
             pull(*n_up)
         pull(*n_down)
-        take_sides(event, both)
 
         def halo(m, carry):
             if both:
-                corr[m, 0] = replace(NDH[m] * NB[m], HR[event, 0], m, 0)
-            corr[m, PLANES + 1] = replace(NDH[m] * NA[sweep, m], HR[event, 1], m, 0)
+                corr[m, 0] = NDH[m] * NB[m]
+            corr[m, PLANES + 1] = NDH[m] * NA[sweep, m]
             return carry
 
         lax.fori_loop(0, macros, halo, 0)
+        gather.third()
+        gather.finish()
+        (extra,) = mates(buf, (0,))
+        event = 1 + 2 * sweep
+        HS[event, 0] = INVP[3] * (buf[row, 0] + extra)
+        up_, down_ = sides_message(event, False)
+        if both:
+            push(*up_)
+        push(*down_)
+
+        def own(m, carry):
+            for p in range(PLANES):
+                corr[m, p + 1] = replace(corr[m, p + 1], HS[event, 0], m, p)
+            return carry
+
+        lax.fori_loop(0, macros, own, 0)
+        if both:
+            pull(*up_)
+        pull(*down_)
+
+        def halo_sides(m, carry):
+            if both:
+                corr[m, 0] = replace(corr[m, 0], HR[event, 0, 0], m, PLANES - 1)
+            corr[m, PLANES + 1] = replace(corr[m, PLANES + 1], HR[event, 1, 0], m, 0)
+            return carry
+
+        lax.fori_loop(0, macros, halo_sides, 0)
 
     def raised(corr, m, z, t):
         dz = 0 if t in FLAT_TYPES else 1
@@ -677,37 +681,29 @@
     push(*r_up)
     push(*r_down)
 
-    def second_private(m, carry):
-        for t in PRIVATE:
+    def second_all(m, packs):
+        packs = list(packs)
+        for t in range(7):
             for p in range(PLANES):
-                EF[m, POS[t], p + 1] = EF[m, POS[t], p + 1] + inverse(m, t, p) * R[m, POS[t], p]
-        return carry
-
-    lax.fori_loop(0, macros, second_private, 0)
+                v = EF[m, POS[t], p + 1]
+                if t in SHARED:
+                    n = SHARED.index(t)
+                    for s in range(2):
+                        packs[n] = packs[n] + ln.pack(v, s, (m * 2 + s) * 4 + p)
+                EF[m, POS[t], p + 1] = v + inverse(m, t, p) * R[m, POS[t], p]
+        return tuple(packs)
+
     g2.second()
+    packs = lax.fori_loop(0, macros, second_all, (zero,) * 3)
+    for n in range(3):
+        EP[n] = packs[n]
+    pull(*r_up)
+    pull(*r_down)
+    halo_edges(RB, RA, False)
     g2.third()
     g2.finish()
-
-    def second_shared(m, carry):
-        up, down = carry
-        for p in range(PLANES):
-            values = assembled(G2, (0, 1, 2), m, p, [R[m, POS[t], p] for t in SHARED])
-            for n, t in enumerate(SHARED):
-                new = EF[m, POS[t], p + 1] + INVS[m, n, p] * values[n]
-                EF[m, POS[t], p + 1] = new
-                for s in range(2):
-                    if p == PLANES - 1:
-                        up = up + ln.pack(new, s, (m * 2 + s) * 4 + n)
-                    if p == 0 and t == 1:
-                        down = down + ln.pack(new, s, (m * 2 + s) * 4 + n)
-        return up, down
-
-    up, down = lax.fori_loop(0, macros, second_shared, (zero, zero))
-    send_sides(2, up, down)
-    pull(*r_up)
-    pull(*r_down)
-    take_sides(2)
-    halo_edges(2, RB, RA, False)
+    extra = mates(G2, (0, 1, 2))
+    edge_sides(2, [EP[n] + INVP[n] * (G2[row, n] + extra[n]) for n in range(3)])
     node_round(1, g3, G3, C2, False)
 
     def finish(m, carry):
@@ -761,11 +757,11 @@
                 tiles(m, 7, 4), tiles(m, 7, 6), tiles(m, 7, 4),
                 tiles(m, 7), tiles(m, 3), tiles(m, 7), tiles(m, 3),
                 tiles(2, m, 4), tiles(m), tiles(2, m), tiles(m, 6), tiles(m, 6),
-                tiles(m, 15), tiles(m, 7), tiles(m, 3), tiles(m, 3, 4), tiles(m), tiles(m, 2, 4), tiles(4),
-                pltpu.VMEM((m,) + TILE, jnp.int32), tiles(m, 4),
+                tiles(m, 15), tiles(m, 7), tiles(m, 3), tiles(4), tiles(m), tiles(m), tiles(3),
+                pltpu.VMEM((m,) + TILE, jnp.int32),
                 tiles(rows, 3), tiles(rows, 1), tiles(rows, 3), tiles(rows, 1),
                 pltpu.VMEM((rows,) + TILE, jnp.int32),
-                tiles(4, 2), tiles(4, 2),
+                tiles(4, 3), tiles(4, 2, 3),
                 pltpu.VMEM((macros, types, split, planes, 128), jnp.float32),
                 pltpu.VMEM((128, 128), jnp.int32),
                 pltpu.VMEM((128, 128), jnp.int32),

time: 97.4 us -> 95.7 us (0.983)
  Pallas kernels: 94 us -> 92.4 us
    pallas_call x1, Pallas kernels: 94 us -> 92.4 us  [local(): pl.pallas_call(functools.partial(kernel, side, n_sub, macros, zones), out...]
where the time goes in v2:
time: 95.7 us; the launch traced here: 95.5 us
  Pallas kernels  92.4 us (97%)
  local copies, waits for them, and re-layouts  2.48 us (3%)
    pallas_call x1, Pallas kernels, local(): pl.pallas_call(functools.partial(kernel, side, n_sub, macros, zones), out...  92.4 us
    unnamed x4, local copies, waits for them, and re-layouts  2.48 us

profile of v2, /device:TPU:1, one launch (start us, length us, event | category | flops | bytes accessed | tf_op | source)
XLA Modules:
  0.0 95.5 jit_solution(3333452274168228948)
XLA Ops:
  0.6 92.4 %shard_map.77 = (f32[4,7,8,4,128]{4,3,2,1,0:T(4,128)}, f32[4,8,4,128]{3,2,1,0:T(4,128)}) custom-call(f32[4,7,8,4,128]{4,3,2,1,0:T(4,128)} %bitcast.15, s32[8,4,128]{2,1,0:T(4,128)} %bitcast.17, s32[1,32]{1,0:T(1,128)} %od_v.1, s32[1,32]{1,0:T(1,128)} %od_v.1, s32[1,128]{1,0:T(1,128)} %og_v.1, f32[7,16]{1,0:T(8,128)} %bitcast.18, f32[8,16]{1,0:T(8,128)} %bitcast.19), custom_call_target="tpu_custom_call" | custom-call | tf_op jit(solution)/shard_map/pallas_call | solution.py:748
  93.0 0.0 copy-start
  93.0 1.8 %copy.10 = f32[4,7,4,1024]{3,2,1,0:T(4,128)} copy(f32[4,7,4,1024]{3,2,1,0:T(4,128)} %bitcast.14) | data formatting | bytes 917504
  94.9 0.0 copy-done
  94.9 0.6 copy.11
Async XLA Ops:
  93.0 1.9 %copy-start = (f32[4,8,4,128]{3,2,1,0:T(4,128)S(1)}, f32[4,8,4,128]{3,2,1,0:T(4,128)}, u32[]{:S(2)}) copy-start(f32[4,8,4,128]{3,2,1,0:T(4,128)} %get-tuple-element.5) | copy-start | bytes 196612
